TPU v7x, 32 devices: a whole 2x2x4 slice. The times are simulated.
32 devices in a mesh: prow: 4 (over z), pcol: 8 (over y, x, core).
Axes of the slice: x: 2, y: 2, z: 4, core: 2. Of those that a mesh axis runs over, the one named last changes fastest.
Arguments:
- anc_inverse: float32 [2048, 2048], P('pcol', 'prow')
- pattern_one: int32 [8, 4], replicated, may hold values from 0 to 7, as said below
- parents: int32 [8], replicated, may hold values from 0 to 7, as said below
- low_one: float32 [8, 1024, 256], P('pcol', 'prow'), may hold values from -2 to 2
- pivot_one: float32 [8, 256, 256], P('pcol'), may hold values from -4 to 4
- low_two: float32 [8, 1024, 256], P('pcol', 'prow'), may hold values from -2 to 2
- second_scaled_factor: float32 [8, 256, 256], P('pcol'), may hold values from -2 to 2
- second_pivot_inverse: float32 [8, 256, 256], P('pcol'), may hold values from -4 to 4
Outputs:
- column_one: float32 [8, 2048, 256], P('prow', 'pcol')
- diag_one: float32 [8, 256, 256], P('pcol')
- column_two: float32 [8, 2048, 256], P('prow', 'pcol')
- second_parent_inverse: float32 [8, 256, 256], P('pcol')
- second_diagonal_inverse: float32 [8, 256, 256], P('pcol')
Inputs may be any that keep to these rules, and one draw needn't show every extreme that they name: `pattern_one`: entry r of each row names an ancestor of process row r: it lies in r * 2 to r * 2 + 1; for each r, every ancestor of that range is entry r of exactly 4 rows. `parents`: every first-level supernode is the parent of exactly one second-level supernode.
All inputs are finite; a program needn't handle non-finite values.
Results may differ from a plain program's by a relative error of at most 0.000073.
Values sent between devices are 32-bit elements; how exact they have to be, the bound alone decides.
A program may use at most 128 MiB of HBM per device.

v0:
```python
import jax
import jax.numpy as jnp
from jax import lax
from jax.sharding import PartitionSpec as P


def batched(left, right):
    return jnp.einsum("kab,kbd->kad", left, right, precision=lax.Precision.HIGHEST)


def batched_left_t(left, right):
    return jnp.einsum("kba,kbd->kad", left, right, precision=lax.Precision.HIGHEST)


def pick_rows(hit_mask, count):
    total = hit_mask.shape[0]
    keys = jnp.where(hit_mask, 0, total).astype(jnp.int32) + jnp.arange(total, dtype=jnp.int32)
    chosen_rows = jnp.argsort(keys)[:count]
    valid = jnp.take(hit_mask, chosen_rows, axis=0).astype(jnp.float32)[:, None, None]
    return (chosen_rows, valid)


def body(
    anc_inverse,
    pattern_one,
    parents,
    low_one,
    pivot_one,
    low_two,
    second_scaled_factor,
    second_pivot_inverse,
):
    my_row = lax.axis_index("prow")
    my_col = lax.axis_index("pcol")
    row_count = lax.axis_size("prow")
    col_count = lax.axis_size("pcol")
    per_row_anc = col_count // row_count
    supernode_block_width = pivot_one.shape[1]
    per_col_one = pivot_one.shape[0]
    per_col_two = second_scaled_factor.shape[0]
    owned = anc_inverse.shape[1] // supernode_block_width
    zblocks = anc_inverse.reshape(supernode_block_width, owned, supernode_block_width).transpose(
        1, 0, 2
    )
    lowall = lax.all_gather(low_one, "pcol", axis=0, tiled=True)
    total_one = lowall.shape[0]
    owned_slot_list = lax.dynamic_index_in_dim(pattern_one, my_row, 1, keepdims=False)
    chosen = jnp.take(zblocks, owned_slot_list - my_row * owned, axis=0)
    first_terms = batched(chosen, lowall)
    lowsec, topall = (
        lax.all_gather(low_two, "pcol", axis=0, tiled=True),
        lax.all_gather(second_scaled_factor, "pcol", axis=0, tiled=True),
    )
    total_two = lowsec.shape[0]
    pattern_two = jnp.take(pattern_one, parents, axis=0)
    my_slots_two = lax.dynamic_index_in_dim(pattern_two, my_row, 1, keepdims=False)
    chosen_two = jnp.take(zblocks, my_slots_two - my_row * owned, axis=0)
    first_full = -lax.psum(first_terms, "prow")
    share = total_two // row_count
    start = my_row * share
    parents_share = lax.dynamic_slice_in_dim(parents, start, share, 0)
    tops_share = lax.dynamic_slice_in_dim(topall, start, share, 0)
    carried = batched(jnp.take(first_full, parents_share, axis=0), tops_share)
    base_terms = batched(chosen_two, lowsec)
    updated = lax.dynamic_slice_in_dim(base_terms, start, share, 0) + carried
    second_terms = lax.dynamic_update_slice_in_dim(base_terms, updated, start, 0)
    second_full = -lax.psum(second_terms, "prow")
    rows_one, valid_one = pick_rows(owned_slot_list == my_col, total_one // per_row_anc)
    pivot_small = valid_one * batched_left_t(
        jnp.take(lowall, rows_one, axis=0), jnp.take(first_full, rows_one, axis=0)
    )
    pivot_terms = jnp.zeros_like(first_full).at[rows_one].add(pivot_small)
    pivot_part = lax.psum_scatter(pivot_terms, "pcol", scatter_dimension=0, tiled=True)
    pivot_sum = lax.psum(pivot_part, "prow")
    diag_one = pivot_one - pivot_sum
    count_one = first_full.shape[0] // row_count
    column_one = lax.dynamic_slice_in_dim(first_full, my_row * count_one, count_one, 0)
    second_level_count = second_full.shape[0] // row_count
    column_two = lax.dynamic_slice_in_dim(
        second_full, my_row * second_level_count, second_level_count, 0
    )
    rows_two, valid_two = pick_rows(my_slots_two == my_col, total_two // per_row_anc)
    lows_picked = jnp.take(lowsec, rows_two, axis=0)
    parent_picked = jnp.take(first_full, jnp.take(parents, rows_two, axis=0), axis=0)
    cross_small = valid_two * batched_left_t(parent_picked, lows_picked)
    diag_small = valid_two * batched_left_t(lows_picked, jnp.take(second_full, rows_two, axis=0))
    local_parent = parents - my_col * per_col_one
    own_parent = (local_parent >= 0) & (local_parent < per_col_one)
    rows_own, valid_own = pick_rows(own_parent, per_col_two)
    valid_own = valid_own * (my_row == 0).astype(jnp.float32)
    local_picked = jnp.clip(jnp.take(local_parent, rows_own, axis=0), 0, per_col_one - 1)
    picked = jnp.take(diag_one, local_picked, axis=0)
    own_small = valid_own * batched(picked, jnp.take(topall, rows_own, axis=0))
    cross_terms = (
        jnp.zeros_like(second_full).at[rows_two].add(cross_small).at[rows_own].add(own_small)
    )
    diag_terms = jnp.zeros_like(second_full).at[rows_two].add(diag_small)
    part_cross, part_diag = (
        lax.psum_scatter(cross_terms, "pcol", scatter_dimension=0, tiled=True),
        lax.psum_scatter(diag_terms, "pcol", scatter_dimension=0, tiled=True),
    )
    sum_cross, sum_diag = lax.psum((part_cross, part_diag), "prow")
    second_parent_inverse = -sum_cross
    second_diagonal_inverse = (
        second_pivot_inverse
        - batched_left_t(second_scaled_factor, second_parent_inverse)
        - sum_diag
    )
    return (column_one, diag_one, column_two, second_parent_inverse, second_diagonal_inverse)


def solution(mesh):
    placed = (
        P("pcol", "prow"),
        P(),
        P(),
        P("pcol", "prow", None),
        P("pcol", None, None),
        P("pcol", "prow", None),
        P("pcol", None, None),
        P("pcol", None, None),
    )
    return jax.shard_map(
        body,
        mesh=mesh,
        in_specs=placed,
        out_specs=(
            P("prow", "pcol", None),
            P("pcol", None, None),
            P("prow", "pcol", None),
            P("pcol", None, None),
            P("pcol", None, None),
        ),
        check_vma=False,
    )
```

profile of v0, /device:TPU:0, one launch (start us, length us, event | category | flops | bytes accessed | tf_op | source)
XLA Modules:
  0.0 471.5 jit_solution(3958737760766188225)
XLA Ops:
  7.2 0.7 all-gather.4.cloned.1.call-update
  8.0 1.2 copy.34
  9.7 0.7 gather_fusion.3
  10.5 30.0 %all-gather.4.cloned.1.call-done = f32[8,256,256]{2,1,0:T(8,128)} async-done(((f32[1,256,256]{2,1,0:T(8,128)}), f32[8,256,256]{2,1,0:T(8,128)}) %all-gather.4.cloned.1.call-update) | async-done | bytes 2097168 | tf_op jit(solution)/shard_map/all_gather | solution.py:45
  40.4 5.1 %fusion.2 = f32[8,256,256]{2,1,0:T(8,128)} fusion(f32[8,256,256]{2,1,0:T(8,128)} %all-gather.4.cloned.1.call-done, f32[8,256,256]{2,1,0:T(8,128)S(1)} %gather_fusion.3, pred[8]{0:T(512)(128)(4,1)S(1)} %compare_and_fusion.4), kind=kOutput, calls=%fused_computation.17 | convolution fusion | flops 1611137024 | bytes 6291464 | tf_op jit(solution)/shard_map/kab,kbd->kad/dot_general | solution.py:8
  45.6 0.7 all-gather.6.cloned.1.call-update
  47.1 1.0 sort.45
  48.1 0.6 gather_fusion.4
  48.7 1.7 gather_fusion.5
  50.4 81.4 %all-reduce.6.cloned.1.call-done = f32[8,256,256]{2,1,0:T(8,128)} async-done(((f32[8,256,256]{2,1,0:T(8,128)}), f32[8,256,256]{2,1,0:T(8,128)}) %all-reduce.6.cloned.1.call-update) | async-done | bytes 2097168 | tf_op jit(solution)/shard_map/psum | solution.py:58
  131.8 1.8 neg.9
  133.6 1.7 gather_fusion.6
  135.3 4.5 convolution_multiply_fusion.2
  140.0 2.3 scatter_fusion
  142.3 1.3 copy-done.3
  144.8 2.0 gather_fusion.7
  146.9 13.7 %all-gather.6.cloned.1.call-done = f32[8,256,256]{2,1,0:T(8,128)} async-done(((f32[1,256,256]{2,1,0:T(8,128)}), f32[8,256,256]{2,1,0:T(8,128)}) %all-gather.6.cloned.1.call-update) | async-done | bytes 2097168 | tf_op jit(solution)/shard_map/all_gather | solution.py:51
  160.6 5.8 %fusion = f32[8,256,256]{2,1,0:T(8,128)} fusion(f32[8,256,256]{2,1,0:T(8,128)} %all-gather.6.cloned.1.call-done, f32[8,256,256]{2,1,0:T(8,128)} %gather_fusion.7, pred[8]{0:T(512)(128)(4,1)S(1)} %compare_and_fusion.2), kind=kOutput, calls=%fused_computation.15 | convolution fusion | flops 1611137024 | bytes 6291464 | tf_op jit(solution)/shard_map/kab,kbd->kad/dot_general | solution.py:8
  166.9 23.2 %all-gather.8.cloned.1.call-done = f32[8,256,256]{2,1,0:T(8,128)} async-done(((f32[1,256,256]{2,1,0:T(8,128)}), f32[8,256,256]{2,1,0:T(8,128)}) %all-gather.8.cloned.1.call-update) | async-done | bytes 2097168 | tf_op jit(solution)/shard_map/all_gather | solution.py:52
  190.1 2.7 fusion.4
  192.9 41.5 %reduce-scatter.4.cloned.1.call-done = f32[1,256,256]{2,1,0:T(8,128)} async-done(((f32[8,256,256]{2,1,0:T(8,128)}), f32[1,256,256]{2,1,0:T(8,128)}) %reduce-scatter.4.cloned.1.call-update) | async-done | bytes 262160 | tf_op jit(solution)/shard_map/reduce_scatter | solution.py:73
  234.7 1.0 sort.46
  235.6 0.6 gather_fusion.2
  236.3 0.6 gather_fusion.8
  236.9 1.0 sort.47
  238.0 0.6 dynamic-slice.18
  240.5 0.7 and_reduce_fusion
  241.2 2.6 gather_fusion.10
  243.8 1.6 gather_fusion.9
  245.3 4.2 convolution_multiply_fusion.1
  249.8 2.3 scatter_fusion.1
  252.1 79.3 %all-reduce.10.cloned.1.call-done = (f32[1,256,256]{2,1,0:T(8,128)}, f32[8,256,256]{2,1,0:T(8,128)}) async-done(((f32[1,256,256]{2,1,0:T(8,128)}, f32[8,256,256]{2,1,0:T(8,128)}), (f32[1,256,256]{2,1,0:T(8,128)}, f32[8,256,256]{2,1,0:T(8,128)})) %all-reduce.10.cloned.1.call-update) | async-done | bytes 2359312 | tf_op jit(solution)/shard_map/psum | solution.py:74
  331.4 1.1 sub.32
  332.5 2.0 fusion.8
  334.5 1.3 copy-done.1
  335.9 1.8 neg.10
  337.7 1.7 gather_fusion.11
  339.4 4.3 convolution_multiply_fusion
  343.9 1.1 copy-done.8
  345.0 1.2 scatter_fusion.2
  346.2 1.3 copy-done.2
  347.7 28.5 %reduce-scatter.6.cloned.1.call-done = f32[1,256,256]{2,1,0:T(8,128)} async-done(((f32[8,256,256]{2,1,0:T(8,128)}), f32[1,256,256]{2,1,0:T(8,128)}) %reduce-scatter.6.cloned.1.call-update) | async-done | bytes 262160 | tf_op jit(solution)/shard_map/reduce_scatter | solution.py:99
  376.2 44.4 %reduce-scatter.8.cloned.1.call-done = f32[1,256,256]{2,1,0:T(8,128)} async-done(((f32[8,256,256]{2,1,0:T(8,128)}), f32[1,256,256]{2,1,0:T(8,128)}) %reduce-scatter.8.cloned.1.call-update) | async-done | bytes 262160 | tf_op jit(solution)/shard_map/reduce_scatter | solution.py:100
  420.6 1.9 constant_dynamic-slice_fusion.1
  422.5 1.9 constant_dynamic-slice_fusion
  424.3 37.3 %all-reduce.8.cloned.1.call-done = (f32[1,256,256]{2,1,0:T(8,128)}, f32[1,256,256]{2,1,0:T(8,128)}) async-done(((f32[1,256,256]{2,1,0:T(8,128)}, f32[1,256,256]{2,1,0:T(8,128)}), (f32[1,256,256]{2,1,0:T(8,128)}, f32[1,256,256]{2,1,0:T(8,128)})) %all-reduce.8.cloned.1.call-update) | async-done | bytes 524304 | tf_op jit(solution)/shard_map/psum | solution.py:102
  461.6 1.0 neg.11
  462.6 2.3 fusion.10
  (77 shorter events, 4.8 us)
Async XLA Ops:
  7.2 2.3 copy-start.13
  7.2 2.5 copy-start
  7.2 33.2 %all-gather.4.cloned.1.call-start = ((), (), s32[]{:S(2)}) async-start(), calls=%async_computation.3 | async-start | bytes 2359296 | tf_op jit(solution)/shard_map/all_gather | solution.py:45
  7.9 123.9 %all-reduce.6.cloned.1.call-start = ((), (), s32[]{:S(2)}) async-start(), calls=%async_computation.4 | async-start | bytes 4194304 | tf_op jit(solution)/shard_map/psum | solution.py:58
  45.5 3.2 copy-start.7
  45.5 115.0 %all-gather.6.cloned.1.call-start = ((), (), s32[]{:S(2)}) async-start(), calls=%async_computation.6 | async-start | bytes 2359296 | tf_op jit(solution)/shard_map/all_gather | solution.py:51
  46.3 143.9 %all-gather.8.cloned.1.call-start = ((), (), s32[]{:S(2)}) async-start(), calls=%async_computation.7 | async-start | bytes 2359296 | tf_op jit(solution)/shard_map/all_gather | solution.py:52
  46.9 187.5 %reduce-scatter.4.cloned.1.call-start = ((), (), s32[]{:S(2)}) async-start(), calls=%async_computation.5 | async-start | bytes 2359296 | tf_op jit(solution)/shard_map/reduce_scatter | solution.py:73
  133.6 1.7 copy-start.4
  142.3 1.3 copy-start.3
  143.7 187.7 %all-reduce.10.cloned.1.call-start = ((), (), s32[]{:S(2)}) async-start(), calls=%async_computation.11 | async-start | bytes 4718592 | tf_op jit(solution)/shard_map/psum | solution.py:74
  146.9 19.5 %copy-start.5 = (f32[8,256,256]{2,1,0:T(8,128)S(1)}, f32[8,256,256]{2,1,0:T(8,128)}, u32[]{:S(2)}) copy-start(f32[8,256,256]{2,1,0:T(8,128)} %copy-done.4) | copy-start | bytes 6291460
  192.9 47.6 %copy-start.14 = (s32[3]{0:T(128)S(1)}, s32[3]{0:T(128)}, u32[]{:S(2)}) copy-start(s32[3]{0:T(128)} %constant.171.clone.1) | copy-start | bytes 40
  234.4 141.8 %reduce-scatter.6.cloned.1.call-start = ((), (), s32[]{:S(2)}) async-start(), calls=%async_computation.8 | async-start | bytes 2359296 | tf_op jit(solution)/shard_map/reduce_scatter | solution.py:99
  332.5 5.2 %copy-start.9 = (f32[1,256,256]{2,1,0:T(8,128)}, f32[1,256,256]{2,1,0:T(8,128)S(1)}, u32[]{:S(2)}) copy-start(f32[1,256,256]{2,1,0:T(8,128)S(1)} %sub.32) | copy-start | bytes 786436
  334.5 1.3 copy-start.1
  335.9 84.7 %reduce-scatter.8.cloned.1.call-start = ((), (), s32[]{:S(2)}) async-start(), calls=%async_computation.9 | async-start | bytes 2359296 | tf_op jit(solution)/shard_map/reduce_scatter | solution.py:100
  337.7 1.7 copy-start.6
  343.7 1.3 copy-start.8
  346.2 1.3 copy-start.2
  347.6 115.0 %copy-start.10 = (f32[1,256,256]{2,1,0:T(8,128)S(1)}, f32[1,256,256]{2,1,0:T(8,128)}, u32[]{:S(2)}) copy-start(f32[1,256,256]{2,1,0:T(8,128)} %param.22) | copy-start | bytes 786436
  347.6 115.0 %copy-start.12 = (f32[1,256,256]{2,1,0:T(8,128)S(1)}, f32[1,256,256]{2,1,0:T(8,128)}, u32[]{:S(2)}) copy-start(f32[1,256,256]{2,1,0:T(8,128)} %param.23) | copy-start | bytes 786436
  347.6 114.0 %all-reduce.8.cloned.1.call-start = ((), (), s32[]{:S(2)}) async-start(), calls=%async_computation.10 | async-start | bytes 1048576 | tf_op jit(solution)/shard_map/psum | solution.py:102
  462.6 2.4 copy-start.11
Sparse Core Ops, SparseCore 0:
  9.9 30.4 all-gather.3
  45.7 86.1 all-reduce.5
  133.7 26.8 all-gather.5
  162.3 27.7 all-gather.7
  193.3 41.0 reduce-scatter.3
  236.7 94.6 all-reduce.9
  336.0 40.1 reduce-scatter.5
  379.5 41.0 reduce-scatter.7
  423.0 38.6 all-reduce.7
where the time goes:
time: 472 us
  waiting for transfers between devices  381 us (81%)
  matrix products  31 us (7%)
  local copies, waits for them, and re-layouts  27 us (6%)
  other arithmetic  16 us (3%)
  between operations  15.6 us (3%)
    psum x1, waiting for transfers between devices, body(): first_full = -lax.psum(first_terms, 'prow')  81.4 us
    psum x1, waiting for transfers between devices, body(): pivot_sum = lax.psum(pivot_part, 'prow')  79.3 us
    reduce_scatter x1, waiting for transfers between devices, body(): lax.psum_scatter(diag_terms, 'pcol', scatter_dimension=0, tiled=True)  44.4 us
    reduce_scatter x1, waiting for transfers between devices, body(): lax.psum_scatter(pivot_terms, 'pcol', scatter_dimension=0, tiled=True)  41.5 us
    psum x1, waiting for transfers between devices, body(): sum_cross, sum_diag = lax.psum((part_cross, part_diag), 'prow')  37.3 us
    all_gather x1, waiting for transfers between devices, body(): lowall = lax.all_gather(low_one, 'pcol', axis=0, tiled=True)  30 us
    reduce_scatter x1, waiting for transfers between devices, body(): lax.psum_scatter(cross_terms, 'pcol', scatter_dimension=0, tiled=True)  28.5 us
    all_gather x1, waiting for transfers between devices, body(): lax.all_gather(second_scaled_factor, 'pcol', axis=0, tiled=True)  23.2 us
  transfers between devices with their start and end apart: 9, of which 9 were waited for; matrix products, arithmetic and copies ran while one was open for 12% of the time, Pallas kernels for 0%

commit v1 on v0

--- a/solution.py
+++ b/solution.py
@@ -55,7 +55,7 @@
     pattern_two = jnp.take(pattern_one, parents, axis=0)
     my_slots_two = lax.dynamic_index_in_dim(pattern_two, my_row, 1, keepdims=False)
     chosen_two = jnp.take(zblocks, my_slots_two - my_row * owned, axis=0)
-    first_full = -lax.psum(first_terms, "prow")
+    first_full = -jnp.sum(lax.all_gather(first_terms, "prow"), axis=0)
     share = total_two // row_count
     start = my_row * share
     parents_share = lax.dynamic_slice_in_dim(parents, start, share, 0)

time: 472 us -> 535 us (1.13)
  waiting for transfers between devices: 381 us -> 438 us
  other arithmetic: 16 us -> 21.7 us
    all_gather x0 -> x1, waiting for transfers between devices: none -> 145 us  [body(): first_full = -jnp.sum(lax.all_gather(first_terms, 'prow'), axis=0)]
    psum x1 -> x0, waiting for transfers between devices: 81.4 us -> none  [body(): first_full = -lax.psum(first_terms, 'prow')]
    all_gather x1, waiting for transfers between devices: 13.7 us -> 7.1 us  [body(): lax.all_gather(low_two, 'pcol', axis=0, tiled=True)]
    reduce_sum x0 -> x1, other arithmetic: none -> 5.59 us  [body(): first_full = -jnp.sum(lax.all_gather(first_terms, 'prow'), axis=0)]
where the time goes in v1:
time: 535 us; the launch traced here: 534 us
  waiting for transfers between devices  438 us (82%)
  matrix products  30.9 us (6%)
  local copies, waits for them, and re-layouts  27.1 us (5%)
  other arithmetic  21.7 us (4%)
  between operations  15.6 us (3%)
    all_gather x1, waiting for transfers between devices, body(): first_full = -jnp.sum(lax.all_gather(first_terms, 'prow'), axis=0)  145 us
    psum x1, waiting for transfers between devices, body(): pivot_sum = lax.psum(pivot_part, 'prow')  79.3 us
    reduce_scatter x1, waiting for transfers between devices, body(): lax.psum_scatter(diag_terms, 'pcol', scatter_dimension=0, tiled=True)  44.4 us
    reduce_scatter x1, waiting for transfers between devices, body(): lax.psum_scatter(pivot_terms, 'pcol', scatter_dimension=0, tiled=True)  41.6 us
    psum x1, waiting for transfers between devices, body(): sum_cross, sum_diag = lax.psum((part_cross, part_diag), 'prow')  37.3 us
    all_gather x1, waiting for transfers between devices, body(): lowall = lax.all_gather(low_one, 'pcol', axis=0, tiled=True)  30 us
    reduce_scatter x1, waiting for transfers between devices, body(): lax.psum_scatter(cross_terms, 'pcol', scatter_dimension=0, tiled=True)  28.5 us
    all_gather x1, waiting for transfers between devices, body(): lax.all_gather(second_scaled_factor, 'pcol', axis=0, tiled=True)  23.3 us
  transfers between devices with their start and end apart: 9, of which 9 were waited for; matrix products, arithmetic and copies ran while one was open for 12% of the time, Pallas kernels for 0%

profile of v1, /device:TPU:0, one launch (start us, length us, event | category | flops | bytes accessed | tf_op | source)
XLA Modules:
  0.0 534.2 jit_solution(9116349264523007068)
XLA Ops:
  7.2 0.7 all-gather.6.cloned.1.call-update
  8.0 1.2 copy.34
  9.7 0.7 gather_fusion.3
  10.5 30.0 %all-gather.6.cloned.1.call-done = f32[8,256,256]{2,1,0:T(8,128)} async-done(((f32[1,256,256]{2,1,0:T(8,128)}), f32[8,256,256]{2,1,0:T(8,128)}) %all-gather.6.cloned.1.call-update) | async-done | bytes 2097168 | tf_op jit(solution)/shard_map/all_gather | solution.py:45
  40.4 5.1 fusion.2
  45.6 0.7 all-gather.8.cloned.1.call-update
  47.1 1.0 sort.45
  48.1 0.6 gather_fusion.4
  48.8 1.6 gather_fusion.5
  50.3 145.0 %all-gather.12.cloned.1.call-done = f32[32,256,256]{2,1,0:T(8,128)} async-done(((f32[8,256,256]{2,1,0:T(8,128)}), f32[32,256,256]{2,1,0:T(8,128)}) %all-gather.12.cloned.1.call-update) | async-done | bytes 8388624 | tf_op jit(solution)/shard_map/all_gather | solution.py:58
  195.4 5.6 %reduce_sum.9 = f32[8,256,256]{2,1,0:T(8,128)} reduce(f32[4,8,256,256]{3,2,1,0:T(8,128)} %bitcast.42, f32[]{:T(128)} %constant.163.clone.1), dimensions={0}, to_apply=%region_0.2 | reduce | flops 1572864 | bytes 10485764 | tf_op jit(solution)/shard_map/reduce_sum | solution.py:58
  200.9 1.8 neg.9
  202.8 1.8 gather_fusion.6
  204.6 4.5 convolution_multiply_fusion.2
  209.3 2.3 scatter_fusion
  211.6 1.3 copy-done.3
  214.0 2.0 gather_fusion.7
  216.2 7.1 %all-gather.8.cloned.1.call-done = f32[8,256,256]{2,1,0:T(8,128)} async-done(((f32[1,256,256]{2,1,0:T(8,128)}), f32[8,256,256]{2,1,0:T(8,128)}) %all-gather.8.cloned.1.call-update) | async-done | bytes 2097168 | tf_op jit(solution)/shard_map/all_gather | solution.py:51
  223.3 5.7 %fusion = f32[8,256,256]{2,1,0:T(8,128)} fusion(f32[8,256,256]{2,1,0:T(8,128)} %all-gather.8.cloned.1.call-done, f32[8,256,256]{2,1,0:T(8,128)} %gather_fusion.7, pred[8]{0:T(512)(128)(4,1)S(1)} %compare_and_fusion.2), kind=kOutput, calls=%fused_computation.15 | convolution fusion | flops 1611137024 | bytes 6291464 | tf_op jit(solution)/shard_map/kab,kbd->kad/dot_general | solution.py:8
  229.6 23.3 %all-gather.10.cloned.1.call-done = f32[8,256,256]{2,1,0:T(8,128)} async-done(((f32[1,256,256]{2,1,0:T(8,128)}), f32[8,256,256]{2,1,0:T(8,128)}) %all-gather.10.cloned.1.call-update) | async-done | bytes 2097168 | tf_op jit(solution)/shard_map/all_gather | solution.py:52
  252.8 2.7 fusion.4
  255.5 41.6 %reduce-scatter.4.cloned.1.call-done = f32[1,256,256]{2,1,0:T(8,128)} async-done(((f32[8,256,256]{2,1,0:T(8,128)}), f32[1,256,256]{2,1,0:T(8,128)}) %reduce-scatter.4.cloned.1.call-update) | async-done | bytes 262160 | tf_op jit(solution)/shard_map/reduce_scatter | solution.py:73
  297.3 1.0 sort.46
  298.3 0.6 gather_fusion.2
  298.9 0.6 gather_fusion.8
  299.6 1.0 sort.47
  303.1 0.7 and_reduce_fusion
  303.8 2.6 gather_fusion.10
  306.4 1.6 gather_fusion.9
  308.1 4.2 convolution_multiply_fusion.1
  312.4 2.3 scatter_fusion.1
  314.8 79.3 %all-reduce.7.cloned.1.call-done = (f32[1,256,256]{2,1,0:T(8,128)}, f32[8,256,256]{2,1,0:T(8,128)}) async-done(((f32[1,256,256]{2,1,0:T(8,128)}, f32[8,256,256]{2,1,0:T(8,128)}), (f32[1,256,256]{2,1,0:T(8,128)}, f32[8,256,256]{2,1,0:T(8,128)})) %all-reduce.7.cloned.1.call-update) | async-done | bytes 2359312 | tf_op jit(solution)/shard_map/psum | solution.py:74
  394.1 1.1 sub.32
  395.2 2.0 fusion.8
  397.2 1.3 copy-done.1
  398.6 1.8 neg.10
  400.4 1.7 gather_fusion.11
  402.1 4.3 convolution_multiply_fusion
  406.6 1.1 copy-done.8
  407.7 1.2 scatter_fusion.2
  408.9 1.3 copy-done.2
  410.3 28.5 %reduce-scatter.6.cloned.1.call-done = f32[1,256,256]{2,1,0:T(8,128)} async-done(((f32[8,256,256]{2,1,0:T(8,128)}), f32[1,256,256]{2,1,0:T(8,128)}) %reduce-scatter.6.cloned.1.call-update) | async-done | bytes 262160 | tf_op jit(solution)/shard_map/reduce_scatter | solution.py:99
  438.8 44.4 %reduce-scatter.8.cloned.1.call-done = f32[1,256,256]{2,1,0:T(8,128)} async-done(((f32[8,256,256]{2,1,0:T(8,128)}), f32[1,256,256]{2,1,0:T(8,128)}) %reduce-scatter.8.cloned.1.call-update) | async-done | bytes 262160 | tf_op jit(solution)/shard_map/reduce_scatter | solution.py:100
  483.3 1.9 constant_dynamic-slice_fusion.1
  485.2 1.9 constant_dynamic-slice_fusion
  487.0 37.3 %all-reduce.5.cloned.1.call-done = (f32[1,256,256]{2,1,0:T(8,128)}, f32[1,256,256]{2,1,0:T(8,128)}) async-done(((f32[1,256,256]{2,1,0:T(8,128)}, f32[1,256,256]{2,1,0:T(8,128)}), (f32[1,256,256]{2,1,0:T(8,128)}, f32[1,256,256]{2,1,0:T(8,128)})) %all-reduce.5.cloned.1.call-update) | async-done | bytes 524304 | tf_op jit(solution)/shard_map/psum | solution.py:102
  524.3 1.0 neg.11
  525.3 2.3 fusion.10
  (78 shorter events, 5.4 us)
Async XLA Ops:
  7.2 2.3 copy-start.13
  7.2 2.5 copy-start
  7.2 33.2 %all-gather.6.cloned.1.call-start = ((), (), s32[]{:S(2)}) async-start(), calls=%async_computation.3 | async-start | bytes 2359296 | tf_op jit(solution)/shard_map/all_gather | solution.py:45
  7.9 187.4 %all-gather.12.cloned.1.call-start = ((), (), s32[]{:S(2)}) async-start(), calls=%async_computation.9 | async-start | bytes 10485760 | tf_op jit(solution)/shard_map/all_gather | solution.py:58
  45.5 3.2 copy-start.7
  45.6 177.7 %all-gather.8.cloned.1.call-start = ((), (), s32[]{:S(2)}) async-start(), calls=%async_computation.5 | async-start | bytes 2359296 | tf_op jit(solution)/shard_map/all_gather | solution.py:51
  46.3 206.5 %all-gather.10.cloned.1.call-start = ((), (), s32[]{:S(2)}) async-start(), calls=%async_computation.6 | async-start | bytes 2359296 | tf_op jit(solution)/shard_map/all_gather | solution.py:52
  46.9 250.2 %reduce-scatter.4.cloned.1.call-start = ((), (), s32[]{:S(2)}) async-start(), calls=%async_computation.4 | async-start | bytes 2359296 | tf_op jit(solution)/shard_map/reduce_scatter | solution.py:73
  202.8 1.8 copy-start.4
  211.6 1.3 copy-start.3
  212.9 181.2 %all-reduce.7.cloned.1.call-start = ((), (), s32[]{:S(2)}) async-start(), calls=%async_computation.11 | async-start | bytes 4718592 | tf_op jit(solution)/shard_map/psum | solution.py:74
  216.1 12.8 %copy-start.5 = (f32[8,256,256]{2,1,0:T(8,128)S(1)}, f32[8,256,256]{2,1,0:T(8,128)}, u32[]{:S(2)}) copy-start(f32[8,256,256]{2,1,0:T(8,128)} %copy-done.4) | copy-start | bytes 6291460
  255.5 47.6 %copy-start.14 = (s32[3]{0:T(128)S(1)}, s32[3]{0:T(128)}, u32[]{:S(2)}) copy-start(s32[3]{0:T(128)} %constant.172.clone.1) | copy-start | bytes 40
  297.1 141.8 %reduce-scatter.6.cloned.1.call-start = ((), (), s32[]{:S(2)}) async-start(), calls=%async_computation.7 | async-start | bytes 2359296 | tf_op jit(solution)/shard_map/reduce_scatter | solution.py:99
  395.2 5.2 copy-start.9
  397.2 1.3 copy-start.1
  398.6 84.7 %reduce-scatter.8.cloned.1.call-start = ((), (), s32[]{:S(2)}) async-start(), calls=%async_computation.8 | async-start | bytes 2359296 | tf_op jit(solution)/shard_map/reduce_scatter | solution.py:100
  400.4 1.7 copy-start.6
  406.4 1.3 copy-start.8
  408.9 1.3 copy-start.2
  410.3 115.0 %copy-start.10 = (f32[1,256,256]{2,1,0:T(8,128)S(1)}, f32[1,256,256]{2,1,0:T(8,128)}, u32[]{:S(2)}) copy-start(f32[1,256,256]{2,1,0:T(8,128)} %param.22) | copy-start | bytes 786436
  410.3 115.0 %copy-start.12 = (f32[1,256,256]{2,1,0:T(8,128)S(1)}, f32[1,256,256]{2,1,0:T(8,128)}, u32[]{:S(2)}) copy-start(f32[1,256,256]{2,1,0:T(8,128)} %param.23) | copy-start | bytes 786436
  410.3 114.0 %all-reduce.5.cloned.1.call-start = ((), (), s32[]{:S(2)}) async-start(), calls=%async_computation.10 | async-start | bytes 1048576 | tf_op jit(solution)/shard_map/psum | solution.py:102
  525.3 2.4 copy-start.11
Sparse Core Ops, SparseCore 0:
  9.9 30.4 all-gather.5
  45.7 149.6 all-gather.11
  197.2 25.9 all-gather.7
  225.0 27.7 all-gather.9
  255.9 41.0 reduce-scatter.3
  299.4 94.6 all-reduce.6
  398.7 40.1 reduce-scatter.5
  442.1 41.0 reduce-scatter.7
  485.7 38.6 all-reduce.4
